TPU v7x, 256 devices: a whole 4x4x8 slice. The times are simulated.
256 devices in a mesh: tm: 8 (over y, x_hi), lon: 32 (over x_lo, z, core).
Axes of the slice: x: 4 (x_hi: 2, x_lo: 2; x = x_hi * 2 + x_lo), y: 4, z: 8, core: 2. Of those that a mesh axis runs over, the one named last changes fastest.
Arguments:
- frames: bfloat16 [64, 16, 24, 4096], P(None, 'tm', None, 'lon'), may hold values from -6 to 6
- cotangent: bfloat16 [64, 16, 24, 4096], P(None, 'tm', None, 'lon'), may hold values from -6 to 6
- w_space: bfloat16 [3, 3, 64, 64], replicated, may hold values from -0.25 to 0.25
- w_time: bfloat16 [3, 64, 64], replicated, may hold values from -0.4375 to 0.4375
Outputs:
- grad_frames: bfloat16 [64, 16, 24, 4096], P(None, 'tm', None, 'lon')
- grad_space: float32 [3, 3, 64, 64], replicated
- grad_time: float32 [3, 64, 64], replicated
All inputs are finite; a program needn't handle non-finite values.
Results may differ from a plain program's by a relative error of at most 0.0049.
Values may be sent and summed in bfloat16 or wider, within the bound.
No kernel may reach another device: no remote copies, remote signals or barrier semaphores. Data moves between devices by JAX's collectives and lax.ppermute only.
A program may use at most 64 MiB of HBM per device.

v0:
```python
import math
import jax
import jax.numpy as jnp
from jax import lax
from jax.sharding import PartitionSpec as P


def padded_2(cells, sides, width):
    for axis, dim in sides:
        count = lax.axis_size(axis)
        head = lax.slice_in_dim(cells, 0, width, axis=dim)
        tail = lax.slice_in_dim(cells, cells.shape[dim] - width, cells.shape[dim], axis=dim)
        cells = jnp.concatenate(
            [
                lax.ppermute(tail, axis, [(i, (i + 1) % count) for i in range(count)]),
                cells,
                lax.ppermute(head, axis, [((i + 1) % count, i) for i in range(count)]),
            ],
            axis=dim,
        )
    return cells


def from_behind(value, axis, steps):
    count = lax.axis_size(axis)
    first, last = (max(0, -steps), min(count, count - steps))
    return lax.ppermute(value, axis, [(source, source + steps) for source in range(first, last)])


def silu_slope(pre):
    sigmoid_value = jax.nn.sigmoid(pre)
    return sigmoid_value * (1.0 + pre * (1.0 - sigmoid_value))


def pad_rows(field):
    return jnp.pad(field, ((0, 0), (0, 0), (1, 1), (0, 0)))


def body(frames, cotangent, w_space, w_time):
    channels, frame_count, lat_rows, lon_cols = frames.shape
    contract_last = (((1,), (1,)), ((), ()))
    contract_first = (((0,), (0,)), ((), ()))
    padded = pad_rows(padded_2(frames, (("lon", 3),), 1))
    later_frames = from_behind(cotangent, "tm", -1)
    later_ext = jnp.concatenate([cotangent, later_frames], axis=1)
    pre = None
    for i in range(3):
        for j in range(3):
            window = padded[:, :, i : i + lat_rows, j : j + lon_cols].reshape(channels, -1)
            term = jnp.dot(w_space[i, j], window, preferred_element_type=jnp.float32)
            pre = term if pre is None else pre + term
    act = jax.nn.silu(pre).astype(jnp.bfloat16)
    upstream = None
    for k in range(3):
        later_k = later_ext[:, k : k + frame_count].reshape(channels, -1)
        term = lax.dot_general(
            w_time[k], later_k, contract_first, preferred_element_type=jnp.float32
        )
        upstream = term if upstream is None else upstream + term
    tm_terms = []
    act_grid = act.reshape(channels, frame_count, lat_rows, lon_cols)
    earlier = from_behind(act_grid, "tm", 1)
    act_ext = jnp.concatenate([earlier, act_grid], axis=1)
    cot_flat = cotangent.reshape(channels, -1)
    for k in range(3):
        window = act_ext[:, 2 - k : 2 - k + frame_count].reshape(channels, -1)
        tm_terms.append(
            lax.dot_general(cot_flat, window, contract_last, preferred_element_type=jnp.float32)
        )
    grad_tm = jnp.stack(tm_terms)
    dpre = (upstream * silu_slope(pre)).astype(jnp.bfloat16)
    dpre_grid = dpre.reshape(channels, frame_count, lat_rows, lon_cols)
    dpad = pad_rows(padded_2(dpre_grid, (("lon", 3),), 1))
    sp_terms = []
    for i in range(3):
        for j in range(3):
            window = padded[:, :, i : i + lat_rows, j : j + lon_cols].reshape(channels, -1)
            sp_terms.append(
                lax.dot_general(dpre, window, contract_last, preferred_element_type=jnp.float32)
            )
    grad_sp = jnp.stack(sp_terms).reshape(3, 3, channels, channels)
    back = None
    for i in range(3):
        for j in range(3):
            window = dpad[:, :, 2 - i : 2 - i + lat_rows, 2 - j : 2 - j + lon_cols].reshape(
                channels, -1
            )
            term = lax.dot_general(
                w_space[i, j], window, contract_first, preferred_element_type=jnp.float32
            )
            back = term if back is None else back + term
    grad_frames = back.astype(jnp.bfloat16).reshape(channels, frame_count, lat_rows, lon_cols)
    grad_sp, grad_tm = lax.psum((grad_sp, grad_tm), ("tm", "lon"))
    total_cells = frame_count * lax.axis_size("tm") * lat_rows * lon_cols * lax.axis_size("lon")
    scale = 1.0 / math.sqrt(total_cells)
    return (grad_frames, grad_sp * scale, grad_tm * scale)


def solution(mesh):
    return jax.shard_map(
        body,
        mesh=mesh,
        in_specs=(P(None, "tm", None, "lon"), P(None, "tm", None, "lon"), P(), P()),
        out_specs=(P(None, "tm", None, "lon"), P(), P()),
        check_vma=False,
    )
```

profile of v0, /device:TPU:1, one launch (start us, length us, event | category | flops | bytes accessed | tf_op | source)
XLA Modules:
  0.0 309.6 jit_solution(8349422694415326540)
XLA Ops:
  7.2 1.7 fusion.141
  9.0 0.7 copy.31
  9.7 3.1 collective-permute-start.1
  12.7 0.7 copy.32
  13.7 1.5 collective-permute-start
  15.9 0.7 collective-permute-done.2
  17.3 1.9 fusion.13
  19.1 0.9 pad_maximum_fusion.3
  20.0 1.8 fusion.139
  24.7 0.8 multiply_convert_fusion
  25.6 1.1 copy.24
  26.7 5.7 %collective-permute-start.5 = (bf16[64,2,24,128]{3,0,2,1:T(8,128)(2,1)}, bf16[64,2,24,128]{3,0,2,1:T(8,128)(2,1)}, u32[]{:S(2)}, u32[]{:S(2)}) collective-permute-start(bf16[64,2,24,128]{3,0,2,1:T(8,128)(2,1)} %copy.24), channel_id=1, source_target_pairs={{0,32},{32,64},{64,96},{96,128},{128,160},{160,192},{192,224},{1,3... | collective-permute-start | bytes 2359304 | tf_op jit(solution)/shard_map/ppermute | solution.py:27
  32.8 1.1 pad_maximum_fusion.4
  34.7 1.9 fusion.7
  40.0 0.7 copy-done.10
  41.4 5.8 %collective-permute-start.3 = (bf16[64,2,24,1]{0,2,3,1:T(8,128)(2,1)S(1)}, bf16[64,2,24,1]{0,2,3,1:T(8,128)(2,1)S(1)}, u32[]{:S(2)}, u32[]{:S(2)}) collective-permute-start(bf16[64,2,24,1]{0,2,3,1:T(8,128)(2,1)S(1)} %copy.33), channel_id=1, source_target_pairs={{0,1},{1,2},{2,3},{3,4},{4,5},{5,6},{6,7},{7,8},{8,9},{9,10},{10,1... | collective-permute-start | bytes 18440 | tf_op jit(solution)/shard_map/ppermute | solution.py:15
  47.2 0.7 copy.34
  47.9 2.1 fusion.19
  52.0 0.9 copy-done.2
  52.9 2.0 pad_maximum_fusion
  54.9 3.3 %select_maximum_fusion = bf16[64,2,26,130]{3,2,1,0:T(8,128)(2,1)S(1)} fusion(bf16[64,2,24,1]{3,2,1,0:T(8,128)(2,1)} %copy-done.2, bf16[64,2,24,128]{3,2,1,0:T(8,128)(2,1)S(1)} %bitcast.272, bf16[64,2,24,1]{3,2,1,0:T(8,128)(2,1)} %copy-done.1), kind=kLoop, calls=%fused_computation.30 | loop fusion | flops 5191680 | bytes 1664000 | tf_op jit(solution)/shard_map/concatenate | solution.py:13
  58.3 1.5 fusion.28
  59.7 1.5 convolution_bitcast_fusion.5
  61.3 82.8 %psum.15 = f32[3,64,64]{1,2,0:T(8,128)S(1)} all-reduce(f32[3,64,64]{1,2,0:T(8,128)S(1)} %pad_maximum_fusion.5), channel_id=1, replica_groups=mesh['tm'=8,'lon'=32] {'tm','lon'}, use_global_device_ids=true, to_apply=%region_1.2 | all-reduce | flops 12288 | bytes 98304 | tf_op jit(solution)/shard_map/psum | solution.py:93
  144.1 1.8 fusion.138
  147.1 0.7 copy-done.8
  148.2 0.7 copy-done.4
  149.4 0.7 copy-done.7
  151.8 0.7 copy.28
  152.5 1.0 copy.56
  153.5 147.6 %all-reduce.4.cloned.1.call-done = f32[3,3,64,64]{3,2,1,0:T(8,128)} async-done(((f32[3,3,64,64]{3,2,1,0:T(8,128)}), f32[3,3,64,64]{3,2,1,0:T(8,128)}) %all-reduce.4.cloned.1.call-update) | async-done | bytes 147472 | tf_op jit(solution)/shard_map/psum | solution.py:93
  301.1 1.7 broadcast_multiply_fusion
  (66 shorter events, 15.5 us)
Async XLA Ops:
  7.2 293.9 %all-reduce.4.cloned.1.call-start = ((), (), s32[]{:S(2)}) async-start(), calls=%async_computation | async-start | bytes 589824 | tf_op jit(solution)/shard_map/psum | solution.py:93
  8.9 4.8 %copy-start.5 = (bf16[64,2,24,128]{3,2,1,0:T(8,128)(2,1)S(1)}, bf16[64,2,24,128]{3,2,1,0:T(8,128)(2,1)}, u32[]{:S(2)}) copy-start(bf16[64,2,24,128]{3,2,1,0:T(8,128)(2,1)} %param.5) | copy-start | bytes 2359300
  9.0 8.3 %copy-start = (bf16[64,2,24,128]{3,2,1,0:T(8,128)(2,1)S(1)}, bf16[64,2,24,128]{3,2,1,0:T(8,128)(2,1)}, u32[]{:S(2)}) copy-start(bf16[64,2,24,128]{3,2,1,0:T(8,128)(2,1)} %param.4) | copy-start | bytes 2359300
  9.7 5.5 %collective-permute-start.1 = (bf16[64,2,24,1]{0,2,3,1:T(8,128)(2,1)S(1)}, bf16[64,2,24,1]{0,2,3,1:T(8,128)(2,1)S(1)}, u32[]{:S(2)}, u32[]{:S(2)}) collective-permute-start(bf16[64,2,24,1]{0,2,3,1:T(8,128)(2,1)S(1)} %copy.31), channel_id=1, source_target_pairs={{0,1},{1,2},{2,3},{3,4},{4,5},{5,6},{6,7},{7,8},{8,9},{9,10},{10,1... | collective-permute-start | bytes 18440 | tf_op jit(solution)/shard_map/ppermute | solution.py:15
  13.4 3.2 %collective-permute-start.2 = (bf16[64,2,24,1]{0,2,3,1:T(8,128)(2,1)S(1)}, bf16[64,2,24,1]{0,2,3,1:T(8,128)(2,1)S(1)}, u32[]{:S(2)}, u32[]{:S(2)}) collective-permute-start(bf16[64,2,24,1]{0,2,3,1:T(8,128)(2,1)S(1)} %copy.32), channel_id=1, source_target_pairs={{1,0},{2,1},{3,2},{4,3},{5,4},{6,5},{7,6},{8,7},{9,8},{10,9},{11,1... | collective-permute-start | bytes 18440 | tf_op jit(solution)/shard_map/ppermute | solution.py:17
  13.7 19.1 %collective-permute-start = (bf16[64,2,24,128]{3,2,1,0:T(8,128)(2,1)S(1)}, bf16[64,2,24,128]{3,2,1,0:T(8,128)(2,1)}, u32[]{:S(2)}, u32[]{:S(2)}) collective-permute-start(bf16[64,2,24,128]{3,2,1,0:T(8,128)(2,1)S(1)} %copy-done.5), channel_id=1, source_target_pairs={{32,0},{64,32},{96,64},{128,96},{160,128},{192,160},{224,192},{33,... | collective-permute-start | bytes 2359304 | tf_op jit(solution)/shard_map/ppermute | solution.py:27
  20.0 1.8 copy-start.9
  26.7 31.5 %collective-permute-start.5 = (bf16[64,2,24,128]{3,0,2,1:T(8,128)(2,1)}, bf16[64,2,24,128]{3,0,2,1:T(8,128)(2,1)}, u32[]{:S(2)}, u32[]{:S(2)}) collective-permute-start(bf16[64,2,24,128]{3,0,2,1:T(8,128)(2,1)} %copy.24), channel_id=1, source_target_pairs={{0,32},{32,64},{64,96},{96,128},{128,160},{160,192},{192,224},{1,3... | collective-permute-start | bytes 2359304 | tf_op jit(solution)/shard_map/ppermute | solution.py:27
  32.7 1.1 copy-start.11
  36.6 3.0 copy-start.3
  40.0 0.7 copy-start.10
  41.4 8.7 %collective-permute-start.3 = (bf16[64,2,24,1]{0,2,3,1:T(8,128)(2,1)S(1)}, bf16[64,2,24,1]{0,2,3,1:T(8,128)(2,1)S(1)}, u32[]{:S(2)}, u32[]{:S(2)}) collective-permute-start(bf16[64,2,24,1]{0,2,3,1:T(8,128)(2,1)S(1)} %copy.33), channel_id=1, source_target_pairs={{0,1},{1,2},{2,3},{3,4},{4,5},{5,6},{6,7},{7,8},{8,9},{9,10},{10,1... | collective-permute-start | bytes 18440 | tf_op jit(solution)/shard_map/ppermute | solution.py:15
  47.9 3.5 %collective-permute-start.4 = (bf16[64,2,24,1]{0,2,3,1:T(8,128)(2,1)S(1)}, bf16[64,2,24,1]{0,2,3,1:T(8,128)(2,1)S(1)}, u32[]{:S(2)}, u32[]{:S(2)}) collective-permute-start(bf16[64,2,24,1]{0,2,3,1:T(8,128)(2,1)S(1)} %copy.34), channel_id=1, source_target_pairs={{1,0},{2,1},{3,2},{4,3},{5,4},{6,5},{7,6},{8,7},{9,8},{10,9},{11,1... | collective-permute-start | bytes 18440 | tf_op jit(solution)/shard_map/ppermute | solution.py:17
  50.8 1.3 copy-start.1
  52.0 0.9 copy-start.2
  54.9 3.3 %copy-start.6 = (bf16[64,2,24,128]{3,2,1,0:T(8,128)(2,1)S(1)}, bf16[64,2,24,128]{3,2,1,0:T(8,128)(2,1)}, u32[]{:S(2)}) copy-start(bf16[64,2,24,128]{3,2,1,0:T(8,128)(2,1)} %param.5) | copy-start | bytes 2359300
  146.7 1.1 copy-start.8
  147.8 1.1 copy-start.4
  148.9 1.1 copy-start.7
Sparse Core Ops, SparseCore 0:
  50.2 250.8 all-reduce.3
where the time goes:
time: 310 us
  waiting for transfers between devices  149 us (48%)
  blocking collectives  82.8 us (27%)
  matrix products  18.4 us (6%)
  local copies, waits for them, and re-layouts  17.8 us (6%)
  starting transfers between devices  16.4 us (5%)
  between operations  14.5 us (5%)
  other arithmetic  10.8 us (3%)
    psum x1, waiting for transfers between devices, body(): grad_sp, grad_tm = lax.psum((grad_sp, grad_tm), ('tm', 'lon'))  148 us
    psum x1, blocking collectives, body(): grad_sp, grad_tm = lax.psum((grad_sp, grad_tm), ('tm', 'lon'))  82.8 us
    ppermute x2, starting transfers between devices, padded_2(): lax.ppermute(tail, axis, [(i, (i + 1) % count) for i in range(count)])  8.86 us
    unnamed x32, local copies, waits for them, and re-layouts  8.46 us
    concatenate x4, other arithmetic, padded_2(): jnp.concatenate([lax.ppermute(tail, axis, [(i, (i + 1) % count) for i in...  8.03 us
    ppermute x2, starting transfers between devices, from_behind(): lax.ppermute(value, axis, [(source, source + steps) for source in range(f...  7.12 us
  transfers between devices with their start and end apart: 7, of which 3 were waited for; matrix products, arithmetic and copies ran while one was open for 13% of the time, Pallas kernels for 0%

commit v1 on v0

--- a/solution.py
+++ b/solution.py
@@ -3,6 +3,7 @@
 import jax.numpy as jnp
 from jax import lax
 from jax.sharding import PartitionSpec as P
+from jax.lax import psum
 
 
 def padded_2(cells, sides, width):
@@ -90,7 +91,7 @@
             )
             back = term if back is None else back + term
     grad_frames = back.astype(jnp.bfloat16).reshape(channels, frame_count, lat_rows, lon_cols)
-    grad_sp, grad_tm = lax.psum((grad_sp, grad_tm), ("tm", "lon"))
+    grad_sp, grad_tm = psum(psum((grad_sp, grad_tm), "lon"), "tm")
     total_cells = frame_count * lax.axis_size("tm") * lat_rows * lon_cols * lax.axis_size("lon")
     scale = 1.0 / math.sqrt(total_cells)
     return (grad_frames, grad_sp * scale, grad_tm * scale)

time: 310 us -> 358 us (1.15); the launches traced: 310 us -> 353 us
  blocking collectives: 82.8 us -> 143 us
  waiting for transfers between devices: 149 us -> 132 us
    psum x1 -> x2, blocking collectives: 82.8 us -> 143 us  [body(): grad_sp, grad_tm = psum(psum((grad_sp, grad_tm), 'lon'), 'tm')]
    psum x1 -> x2, waiting for transfers between devices: 148 us -> 131 us  [body(): grad_sp, grad_tm = psum(psum((grad_sp, grad_tm), 'lon'), 'tm')]
    unnamed x32 -> x34, local copies, waits for them, and re-layouts: 8.46 us -> 8.47 us
  transfers between devices with their start and end apart: 7 -> 8, of which waited for: 3 -> 4; matrix products, arithmetic and copies ran while one was open for 13% -> 11% of each run, Pallas kernels for 0% -> 0%
where the time goes in v1:
time: 358 us; the launch traced here: 353 us
  blocking collectives  143 us (40%)
  waiting for transfers between devices  132 us (37%)
  local copies, waits for them, and re-layouts  18.6 us (5%)
  matrix products  18.5 us (5%)
  starting transfers between devices  16.4 us (5%)
  between operations  14.6 us (4%)
  other arithmetic  10.8 us (3%)
    psum x2, blocking collectives, body(): grad_sp, grad_tm = psum(psum((grad_sp, grad_tm), 'lon'), 'tm')  143 us
    psum x2, waiting for transfers between devices, body(): grad_sp, grad_tm = psum(psum((grad_sp, grad_tm), 'lon'), 'tm')  131 us
    ppermute x2, starting transfers between devices, padded_2(): lax.ppermute(tail, axis, [(i, (i + 1) % count) for i in range(count)])  8.87 us
    unnamed x34, local copies, waits for them, and re-layouts  8.47 us
    concatenate x4, other arithmetic, padded_2(): jnp.concatenate([lax.ppermute(tail, axis, [(i, (i + 1) % count) for i in...  8.02 us
  transfers between devices with their start and end apart: 8, of which 4 were waited for; matrix products, arithmetic and copies ran while one was open for 11% of the time, Pallas kernels for 0%

profile of v1, /device:TPU:1, one launch (start us, length us, event | category | flops | bytes accessed | tf_op | source)
XLA Modules:
  0.0 353.3 jit_solution(12531043543133433257)
XLA Ops:
  7.2 1.7 fusion.141
  9.0 0.7 copy.31
  9.7 3.1 collective-permute-start.1
  13.7 1.5 collective-permute-start
  15.9 0.7 collective-permute-done.2
  17.3 1.9 fusion.13
  19.1 0.9 pad_maximum_fusion.3
  20.0 1.8 fusion.139
  24.7 0.8 multiply_convert_fusion
  25.6 1.1 copy.24
  26.7 5.6 %collective-permute-start.5 = (bf16[64,2,24,128]{3,0,2,1:T(8,128)(2,1)}, bf16[64,2,24,128]{3,0,2,1:T(8,128)(2,1)}, u32[]{:S(2)}, u32[]{:S(2)}) collective-permute-start(bf16[64,2,24,128]{3,0,2,1:T(8,128)(2,1)} %copy.24), channel_id=1, source_target_pairs={{0,32},{32,64},{64,96},{96,128},{128,160},{160,192},{192,224},{1,3... | collective-permute-start | bytes 2359304 | tf_op jit(solution)/shard_map/ppermute | solution.py:28
  32.8 1.1 pad_maximum_fusion.4
  34.7 1.9 fusion.7
  40.0 0.7 copy-done.11
  41.4 5.8 %collective-permute-start.3 = (bf16[64,2,24,1]{0,2,3,1:T(8,128)(2,1)S(1)}, bf16[64,2,24,1]{0,2,3,1:T(8,128)(2,1)S(1)}, u32[]{:S(2)}, u32[]{:S(2)}) collective-permute-start(bf16[64,2,24,1]{0,2,3,1:T(8,128)(2,1)S(1)} %copy.33), channel_id=1, source_target_pairs={{0,1},{1,2},{2,3},{3,4},{4,5},{5,6},{6,7},{7,8},{8,9},{9,10},{10,1... | collective-permute-start | bytes 18440 | tf_op jit(solution)/shard_map/ppermute | solution.py:16
  48.0 2.1 fusion.19
  52.0 0.9 copy-done.2
  52.9 2.0 pad_maximum_fusion
  54.9 3.3 select_maximum_fusion
  58.2 1.5 fusion.28
  59.7 1.5 convolution_bitcast_fusion.5
  61.3 105.4 %psum.30 = f32[3,64,64]{1,2,0:T(8,128)S(1)} all-reduce(f32[3,64,64]{1,2,0:T(8,128)S(1)} %pad_maximum_fusion.5), channel_id=1, replica_groups=mesh['tm'=8,'lon'=32] {'lon'}, use_global_device_ids=true, to_apply=%region_2.3 | all-reduce | flops 12288 | bytes 98304 | tf_op jit(solution)/shard_map/psum | solution.py:94
  166.7 37.3 %psum.31 = f32[3,64,64]{1,2,0:T(8,128)S(1)} all-reduce(f32[3,64,64]{1,2,0:T(8,128)S(1)} %psum.30), channel_id=1, replica_groups=mesh['tm'=8,'lon'=32] {'tm'}, use_global_device_ids=true, to_apply=%region_3.4 | all-reduce | flops 12288 | bytes 98304 | tf_op jit(solution)/shard_map/psum | solution.py:94
  203.9 2.6 fusion.138
  207.8 0.7 copy-done.9
  208.9 0.7 copy-done.5
  210.0 0.7 copy-done.8
  212.0 0.7 copy.28
  212.8 47.1 %all-reduce.5.cloned.1.call-done = f32[3,3,64,64]{3,2,1,0:T(8,128)} async-done(((f32[3,3,64,64]{3,2,1,0:T(8,128)}), f32[3,3,64,64]{3,2,1,0:T(8,128)}) %all-reduce.5.cloned.1.call-update) | async-done | bytes 147472 | tf_op jit(solution)/shard_map/psum | solution.py:94
  260.4 1.0 copy.56
  261.4 83.4 %all-reduce.7.cloned.1.call-done = f32[3,3,64,64]{3,2,1,0:T(8,128)} async-done(((f32[3,3,64,64]{3,2,1,0:T(8,128)}), f32[3,3,64,64]{3,2,1,0:T(8,128)}) %all-reduce.7.cloned.1.call-update) | async-done | bytes 147472 | tf_op jit(solution)/shard_map/psum | solution.py:94
  344.8 1.7 broadcast_multiply_fusion
  (72 shorter events, 16.9 us)
Async XLA Ops:
  7.2 252.8 %all-reduce.5.cloned.1.call-start = ((), (), s32[]{:S(2)}) async-start(), calls=%async_computation | async-start | bytes 589824 | tf_op jit(solution)/shard_map/psum | solution.py:94
  8.9 4.8 %copy-start.6 = (bf16[64,2,24,128]{3,2,1,0:T(8,128)(2,1)S(1)}, bf16[64,2,24,128]{3,2,1,0:T(8,128)(2,1)}, u32[]{:S(2)}) copy-start(bf16[64,2,24,128]{3,2,1,0:T(8,128)(2,1)} %param.5) | copy-start | bytes 2359300
  9.0 8.3 %copy-start = (bf16[64,2,24,128]{3,2,1,0:T(8,128)(2,1)S(1)}, bf16[64,2,24,128]{3,2,1,0:T(8,128)(2,1)}, u32[]{:S(2)}) copy-start(bf16[64,2,24,128]{3,2,1,0:T(8,128)(2,1)} %param.4) | copy-start | bytes 2359300
  9.7 5.5 %collective-permute-start.1 = (bf16[64,2,24,1]{0,2,3,1:T(8,128)(2,1)S(1)}, bf16[64,2,24,1]{0,2,3,1:T(8,128)(2,1)S(1)}, u32[]{:S(2)}, u32[]{:S(2)}) collective-permute-start(bf16[64,2,24,1]{0,2,3,1:T(8,128)(2,1)S(1)} %copy.31), channel_id=1, source_target_pairs={{0,1},{1,2},{2,3},{3,4},{4,5},{5,6},{6,7},{7,8},{8,9},{9,10},{10,1... | collective-permute-start | bytes 18440 | tf_op jit(solution)/shard_map/ppermute | solution.py:16
  13.4 3.2 collective-permute-start.2
  13.7 19.0 %collective-permute-start = (bf16[64,2,24,128]{3,2,1,0:T(8,128)(2,1)S(1)}, bf16[64,2,24,128]{3,2,1,0:T(8,128)(2,1)}, u32[]{:S(2)}, u32[]{:S(2)}) collective-permute-start(bf16[64,2,24,128]{3,2,1,0:T(8,128)(2,1)S(1)} %copy-done.6), channel_id=1, source_target_pairs={{32,0},{64,32},{96,64},{128,96},{160,128},{192,160},{224,192},{33,... | collective-permute-start | bytes 2359304 | tf_op jit(solution)/shard_map/ppermute | solution.py:28
  20.0 1.8 copy-start.10
  26.7 31.5 %collective-permute-start.5 = (bf16[64,2,24,128]{3,0,2,1:T(8,128)(2,1)}, bf16[64,2,24,128]{3,0,2,1:T(8,128)(2,1)}, u32[]{:S(2)}, u32[]{:S(2)}) collective-permute-start(bf16[64,2,24,128]{3,0,2,1:T(8,128)(2,1)} %copy.24), channel_id=1, source_target_pairs={{0,32},{32,64},{64,96},{96,128},{128,160},{160,192},{192,224},{1,3... | collective-permute-start | bytes 2359304 | tf_op jit(solution)/shard_map/ppermute | solution.py:28
  32.7 1.1 copy-start.12
  36.6 3.0 copy-start.4
  40.0 0.7 copy-start.11
  41.4 8.7 %collective-permute-start.3 = (bf16[64,2,24,1]{0,2,3,1:T(8,128)(2,1)S(1)}, bf16[64,2,24,1]{0,2,3,1:T(8,128)(2,1)S(1)}, u32[]{:S(2)}, u32[]{:S(2)}) collective-permute-start(bf16[64,2,24,1]{0,2,3,1:T(8,128)(2,1)S(1)} %copy.33), channel_id=1, source_target_pairs={{0,1},{1,2},{2,3},{3,4},{4,5},{5,6},{6,7},{7,8},{8,9},{9,10},{10,1... | collective-permute-start | bytes 18440 | tf_op jit(solution)/shard_map/ppermute | solution.py:16
  47.9 3.5 collective-permute-start.4
  50.1 294.7 %all-reduce.7.cloned.1.call-start = ((), (), s32[]{:S(2)}) async-start(), calls=%async_computation.1 | async-start | bytes 589824 | tf_op jit(solution)/shard_map/psum | solution.py:94
  50.8 1.2 copy-start.1
  52.0 0.9 copy-start.2
  54.9 3.3 copy-start.7
  207.3 1.1 copy-start.9
  208.5 1.1 copy-start.5
  209.6 1.1 copy-start.8
  211.6 48.4 %copy-start.3 = (bf16[64,2,24,128]{3,2,1,0:T(8,128)(2,1)S(1)}, bf16[64,2,24,128]{3,2,1,0:T(8,128)(2,1)}, u32[]{:S(2)}) copy-start(bf16[64,2,24,128]{3,2,1,0:T(8,128)(2,1)} %get-tuple-element.9) | copy-start | bytes 2359300
Sparse Core Ops, SparseCore 0:
  50.2 209.6 all-reduce.4
  262.7 81.9 all-reduce.6
